TPU v7x, 512 devices: a whole 4x8x8 slice. The times are simulated.
512 devices in a mesh: ab: 32 (over z, x), cd: 16 (over y, core).
Axes of the slice: x: 4, y: 8, z: 8, core: 2. Of those that a mesh axis runs over, the one named last changes fastest.
Arguments:
- amplitudes: float32 [512, 8192], P('ab', 'cd'), may hold values from -6 to 6
- integrals: float32 [65536, 8192], P('ab', 'cd'), may hold values from -0.125 to 0.125
- ij_pairs: int32 [512, 2], P('cd'), may hold values from 0 to 127
- ab_pairs: int32 [65536, 2], P('ab'), may hold values from 0 to 1535
- eps_occ: float32 [128], replicated, may hold values from -1.5 to -0.3
- eps_vir: float32 [1536], replicated, may hold values from 0.1 to 2.5
Outputs:
- ladder: float32 [512, 65536], P('cd', 'ab')
- update: float32 [512, 65536], P('cd', 'ab')
All inputs are finite; a program needn't handle non-finite values.
Results may differ from a plain program's by a relative error of at most 0.00015.
Values sent between devices are 32-bit elements; how exact they have to be, the bound alone decides.
A program may use at most 64 MiB of HBM per device.

v0:
```python
import jax
import jax.numpy as jnp
from jax import lax
from jax.sharding import PartitionSpec as P


def lookup_energy(indices, energies):
    positions = lax.broadcasted_iota(jnp.int32, (indices.shape[0], energies.shape[0]), 1)
    picked = jnp.where(indices[:, None] == positions, energies[None, :], jnp.float32(0.0))
    return jnp.sum(picked, axis=1)


def contract_rows(row_block, col_block):
    return lax.dot_general(
        row_block,
        col_block,
        (((1,), (1,)), ((), ())),
        precision=lax.Precision.HIGHEST,
        preferred_element_type=jnp.float32,
    )


def on_device(amplitudes, integrals, ij_pairs, ab_pairs, eps_occ, eps_vir):
    partial_value = contract_rows(lax.all_gather(amplitudes, "ab", axis=0, tiled=True), integrals)
    ladder = lax.psum_scatter(partial_value, "cd", scatter_dimension=0, tiled=True)
    first_occ = lookup_energy(ij_pairs[:, 0], eps_occ)[:, None]
    second_occ = lookup_energy(ij_pairs[:, 1], eps_occ)[:, None]
    first_vir = lookup_energy(ab_pairs[:, 0], eps_vir)[None, :]
    second_vir = lookup_energy(ab_pairs[:, 1], eps_vir)[None, :]
    denominator = first_occ + second_occ - first_vir - second_vir
    update = ladder / denominator
    return (ladder, update)


def solution(mesh):
    in_specs = (P("ab", "cd"), P("ab", "cd"), P("cd", None), P("ab", None), P(), P())
    out_specs = (P("cd", "ab"), P("cd", "ab"))
    return jax.shard_map(
        on_device, mesh=mesh, in_specs=in_specs, out_specs=out_specs, check_vma=False
    )
```

profile of v0, /device:TPU:27, one launch (start us, length us, event | category | flops | bytes accessed | tf_op | source)
XLA Modules:
  0.0 179.7 jit_solution(8097404686899207612)
XLA Ops:
  7.2 0.0 all-gather.2.cloned.1.call-start
  7.2 0.7 all-gather.2.cloned.1.call-update
  7.9 0.0 reduce-scatter.2.cloned.1.call-start
  7.9 84.6 %all-gather.2.cloned.1.call-done = f32[512,512]{1,0:T(8,128)} async-done(((f32[16,512]{1,0:T(8,128)}), f32[512,512]{1,0:T(8,128)}) %all-gather.2.cloned.1.call-update) | async-done | bytes 1048592 | tf_op jit(solution)/shard_map/all_gather | solution.py:24
  92.5 10.4 %fusion.1 = f32[512,2048]{1,0:T(8,128)} fusion(f32[512,512]{1,0:T(8,128)} %all-gather.2.cloned.1.call-done, f32[2048,512]{1,0:T(8,128)} %param.7), kind=kOutput, calls=%fused_computation.12 | convolution fusion | flops 6442450944 | bytes 9437184 | tf_op jit(solution)/shard_map/dot_general | solution.py:14
  102.9 0.0 copy-start.1
  102.9 0.0 copy-start.2
  102.9 0.0 copy-start
  102.9 0.0 copy-start.3
  102.9 0.0 reduce-scatter.2.cloned.1.call-update
  102.9 0.6 copy-done.1
  103.5 0.0 copy-done.2
  103.5 0.2 select_reduce_fusion.2
  103.7 0.0 copy-done
  103.8 0.0 copy-done.3
  103.8 3.9 %select_reduce_fusion.1 = (f32[2048]{0:T(1024)S(1)}, f32[2048]{0:T(1024)S(1)}) fusion(f32[1536]{0:T(1024)S(1)} %copy-done.3, s32[2048]{0:T(1024)S(1)} %bitcast.9, s32[2048]{0:T(1024)S(1)} %bitcast.8), kind=kLoop, calls=%fused_computation.2 | loop fusion | flops 18870272 | bytes 38912 | tf_op jit(solution)/shard_map/reduce_sum | solution.py:10
  107.7 63.4 %reduce-scatter.2.cloned.1.call-done = f32[32,2048]{1,0:T(8,128)} async-done(((f32[512,2048]{1,0:T(8,128)}), f32[32,2048]{1,0:T(8,128)}) %reduce-scatter.2.cloned.1.call-update) | async-done | bytes 262160 | tf_op jit(solution)/shard_map/reduce_scatter | solution.py:25
  171.1 1.8 subtract_divide_fusion
  (3 shorter events, 0.0 us)
Async XLA Ops:
  7.2 85.3 %all-gather.2.cloned.1.call-start = ((), (), s32[]{:S(2)}) async-start(), calls=%async_computation.1 | async-start | bytes 1081344 | tf_op jit(solution)/shard_map/all_gather | solution.py:24
  7.9 163.2 %reduce-scatter.2.cloned.1.call-start = ((), (), s32[]{:S(2)}) async-start(), calls=%async_computation.2 | async-start | bytes 4456448 | tf_op jit(solution)/shard_map/reduce_scatter | solution.py:25
  102.9 0.7 copy-start.1
  102.9 0.7 copy-start.2
  102.9 0.9 copy-start
  102.9 0.9 copy-start.3
Sparse Core Ops, SparseCore 0:
  11.2 81.2 all-gather.1
  103.0 67.9 reduce-scatter.1
where the time goes:
time: 180 us
  waiting for transfers between devices  149 us (83%)
  between operations  14.1 us (8%)
  matrix products  10.4 us (6%)
  other arithmetic  5.86 us (3%)
    all_gather x1, waiting for transfers between devices, on_device(): lax.all_gather(amplitudes, 'ab', axis=0, tiled=True)  84.6 us
    reduce_scatter x1, waiting for transfers between devices, on_device(): lax.psum_scatter(partial_value, 'cd', scatter_dimension=0, tiled=True)  63.4 us
    dot_general x1, matrix products, contract_rows(): lax.dot_general(row_block, col_block, (((1,), (1,)), ((), ())), precision...  10.4 us
    reduce_sum x2, other arithmetic, lookup_energy(): return jnp.sum(picked, axis=1)  4.09 us
  transfers between devices with their start and end apart: 2, of which 2 were waited for; matrix products, arithmetic and copies ran while one was open for 2% of the time, Pallas kernels for 0%

commit v1 on v0

--- a/solution.py
+++ b/solution.py
@@ -21,7 +21,12 @@
 
 
 def on_device(amplitudes, integrals, ij_pairs, ab_pairs, eps_occ, eps_vir):
-    partial_value = contract_rows(lax.all_gather(amplitudes, "ab", axis=0, tiled=True), integrals)
+    partial_value = contract_rows(
+        jnp.concatenate(
+            lax.all_to_all(jnp.stack([amplitudes] * lax.axis_size("ab")), "ab", 0, 0), axis=0
+        ),
+        integrals,
+    )
     ladder = lax.psum_scatter(partial_value, "cd", scatter_dimension=0, tiled=True)
     first_occ = lookup_energy(ij_pairs[:, 0], eps_occ)[:, None]
     second_occ = lookup_energy(ij_pairs[:, 1], eps_occ)[:, None]

time: 180 us -> 131 us (0.73)
  the two profiles are of different devices: /device:TPU:27 before, /device:TPU:29 now
where the time goes in v1:
time: 131 us; the launch traced here: 130 us
  waiting for transfers between devices  59 us (45%)
  blocking collectives  39.6 us (30%)
  between operations  14.1 us (11%)
  matrix products  10.1 us (8%)
  other arithmetic  5.86 us (4%)
  local copies, waits for them, and re-layouts  1.54 us (1%)
    reduce_scatter x1, waiting for transfers between devices, on_device(): lax.psum_scatter(partial_value, 'cd', scatter_dimension=0, tiled=True)  58.9 us
    all_to_all x1, blocking collectives, on_device(): lax.all_to_all(jnp.stack([amplitudes] * lax.axis_size('ab')), 'ab', 0, 0)  39.6 us
    dot_general x1, matrix products, contract_rows(): lax.dot_general(row_block, col_block, (((1,), (1,)), ((), ())), precision...  10.1 us
    reduce_sum x2, other arithmetic, lookup_energy(): return jnp.sum(picked, axis=1)  4.09 us
  transfers between devices with their start and end apart: 1, of which 1 were waited for; matrix products, arithmetic and copies ran while one was open for 3% of the time, Pallas kernels for 0%

profile of v1, /device:TPU:29, one launch (start us, length us, event | category | flops | bytes accessed | tf_op | source)
XLA Modules:
  0.0 130.2 jit_solution(6418490993698102634)
XLA Ops:
  7.2 0.0 reduce-scatter.2.cloned.1.call-start
  7.2 0.9 stack.2
  8.1 39.6 %all_to_all.5 = f32[32,16,512]{2,1,0:T(8,128)S(1)} all-to-all(f32[32,16,512]{2,1,0:T(8,128)S(1)} %stack.2), channel_id=1, replica_groups=mesh['ab'=32,'cd'=16] {'ab'}, dimensions={0} | all-to-all | bytes 2097152 | tf_op jit(solution)/shard_map/all_to_all | solution.py:26
  47.7 10.1 %fusion.1 = f32[512,2048]{1,0:T(8,128)} fusion(f32[512,512]{1,0:T(8,128)S(1)} %bitcast.9, f32[2048,512]{1,0:T(8,128)} %param.7), kind=kOutput, calls=%fused_computation.12 | convolution fusion | flops 6442450944 | bytes 9437184 | tf_op jit(solution)/shard_map/dot_general | solution.py:14
  57.8 0.0 copy-start.1
  57.8 0.0 copy-start.2
  57.8 0.0 copy-start
  57.8 0.0 copy-start.3
  57.9 0.0 reduce-scatter.2.cloned.1.call-update
  57.9 0.6 copy-done.1
  58.5 0.0 copy-done.2
  58.5 0.2 select_reduce_fusion.2
  58.7 0.0 copy-done
  58.8 0.0 copy-done.3
  58.8 3.9 %select_reduce_fusion.1 = (f32[2048]{0:T(1024)S(1)}, f32[2048]{0:T(1024)S(1)}) fusion(f32[1536]{0:T(1024)S(1)} %copy-done.3, s32[2048]{0:T(1024)S(1)} %bitcast.11, s32[2048]{0:T(1024)S(1)} %bitcast.10), kind=kLoop, calls=%fused_computation.2 | loop fusion | flops 18870272 | bytes 38912 | tf_op jit(solution)/shard_map/reduce_sum | solution.py:10
  62.7 58.9 %reduce-scatter.2.cloned.1.call-done = f32[32,2048]{1,0:T(8,128)} async-done(((f32[512,2048]{1,0:T(8,128)}), f32[32,2048]{1,0:T(8,128)}) %reduce-scatter.2.cloned.1.call-update) | async-done | bytes 262160 | tf_op jit(solution)/shard_map/reduce_scatter | solution.py:30
  121.6 1.8 %subtract_divide_fusion = f32[32,2048]{1,0:T(8,128)} fusion(f32[32,2048]{1,0:T(8,128)} %reduce-scatter.2.cloned.1.call-done, f32[2048]{0:T(1024)S(1)} %get-tuple-element.3, f32[2048]{0:T(1024)S(1)} %get-tuple-element.2, f32[32]{0:T(128)S(1)} %add.10), kind=kLoop, calls=%fused_computation.4 | loop fusion | flops 196608 | bytes 540800 | tf_op jit(solution)/shard_map/div | solution.py:36
  (3 shorter events, 0.0 us)
Async XLA Ops:
  7.2 114.5 %reduce-scatter.2.cloned.1.call-start = ((), (), s32[]{:S(2)}) async-start(), calls=%async_computation.2 | async-start | bytes 4456448 | tf_op jit(solution)/shard_map/reduce_scatter | solution.py:30
  57.8 0.7 copy-start.1
  57.8 0.7 copy-start.2
  57.8 0.9 copy-start
  57.8 0.9 copy-start.3
Sparse Core Ops, SparseCore 0:
  58.0 63.5 reduce-scatter.1
